TPU v7x, 32 devices: a whole 2x2x4 slice. The times are simulated.
32 devices in a mesh: row: 16 (over z, x, core), col: 2 (over y).
Axes of the slice: x: 2, y: 2, z: 4, core: 2. Of those that a mesh axis runs over, the one named last changes fastest.
Arguments:
- inverse_rows: bfloat16 [2048, 2048], P('row', 'col'), may hold values from -6 to 6
- panel_rows: bfloat16 [2048, 512], P('row', 'col'), may hold values from -0.1875 to 0.1875
- diag_inverse: float32 [512, 512], P('row', 'col'), may hold values from -6 to 6
- pattern: int32 [1, 16], replicated, may hold values 0 or 1
Outputs:
- offdiag: bfloat16 [2048, 512], P('row', 'col')
- diag_block: float32 [512, 512], P('row', 'col')
All inputs are finite; a program needn't handle non-finite values.
Results may differ from a plain program's by a relative error of at most 0.0018.
Values may be sent and summed in bfloat16 or wider, within the bound.
A program may use at most 64 MiB of HBM per device.

v0:
```python
import jax
import jax.numpy as jnp
from jax import lax
from jax.sharding import PartitionSpec as P

BLK = 128
NBR_DEV = 1


def broadcast(array, axis, root):
    mine = lax.axis_index(axis) == root
    return lax.psum(jnp.where(mine, array, jnp.zeros_like(array)), axis)


def shards(inverse_rows, panel_rows, diag_inverse, pattern):
    row_index = lax.axis_index("row")
    col_index = lax.axis_index("col")
    roots_per = lax.axis_size("row") // lax.axis_size("col")
    local_rows = inverse_rows.shape[0]
    half_width = panel_rows.shape[1]
    supernode = col_index // 2
    own_pattern = lax.dynamic_slice(pattern, (supernode, row_index * NBR_DEV), (1, NBR_DEV))
    row_live = jnp.repeat(own_pattern[0], BLK) > 0
    masked = jnp.where(row_live[:, None], panel_rows, jnp.zeros_like(panel_rows))
    whole_rows = lax.all_gather(masked, "col", axis=1, tiled=True)
    full_width = whole_rows.shape[1]
    running = jnp.zeros((local_rows, full_width), jnp.float32)
    for source in range(roots_per):
        received = broadcast(whole_rows, "row", col_index * roots_per + source)
        columns = lax.dynamic_slice_in_dim(inverse_rows, source * local_rows, local_rows, 1)
        running = running + jnp.dot(columns, received, preferred_element_type=jnp.float32)
    column_total = lax.psum_scatter(running, "col", scatter_dimension=1, tiled=True)
    offdiag = jnp.where(row_live[:, None], -column_total, jnp.zeros_like(column_total)).astype(
        jnp.bfloat16
    )
    node_cols = lax.dynamic_slice_in_dim(whole_rows, supernode * 2 * half_width, 2 * half_width, 1)
    partial_term = lax.dot_general(
        node_cols, offdiag, (((0,), (0,)), ((), ())), preferred_element_type=jnp.float32
    )
    summed = lax.psum_scatter(partial_term, "row", scatter_dimension=0, tiled=True)
    return (offdiag, diag_inverse - summed)


def solution(mesh):
    placed = (P("row", "col"), P("row", "col"), P("row", "col"), P())
    return jax.shard_map(
        shards,
        mesh=mesh,
        in_specs=placed,
        out_specs=(P("row", "col"), P("row", "col")),
        check_vma=False,
    )
```

profile of v0, /device:TPU:0, one launch (start us, length us, event | category | flops | bytes accessed | tf_op | source)
XLA Modules:
  0.0 200.6 jit_solution(6880411985263458444)
XLA Ops:
  7.2 0.0 all-reduce.3.cloned.1.call-start
  7.2 0.9 copy.6
  8.2 0.0 copy-start.9
  8.2 0.7 copy-done.9
  8.9 0.6 fusion.10
  9.4 0.7 broadcast_select_fusion.8
  10.1 5.9 %all_gather.3 = bf16[128,512]{0,1:T(8,128)(2,1)S(1)} all-gather(bf16[128,256]{0,1:T(8,128)(2,1)S(1)} %broadcast_select_fusion.8), channel_id=1, replica_groups=mesh['row'=16,'col'=2] {'col'}, dimensions={1}, use_global_device_ids=true | all-gather | bytes 196608 | tf_op jit(solution)/shard_map/all_gather | solution.py:25
  16.0 1.0 broadcast_select_fusion
  17.0 0.0 copy-start
  17.0 0.0 all-reduce.3.cloned.1.call-update
  17.0 0.0 reduce-scatter.3.cloned.1.call-start
  17.1 97.1 %all-reduce.3.cloned.1.call-done = (bf16[128,512]{0,1:T(8,128)(2,1)}, bf16[128,512]{0,1:T(8,128)(2,1)}, bf16[128,512]{0,1:T(8,128)(2,1)}, bf16[128,512]{0,1:T(8,...) async-done(((bf16[128,512]{0,1:T(8,128)(2,1)}, bf16[128,512]{0,1:T(8,128)(2,1)}, ...) | async-done | bytes 1048592 | tf_op jit(solution)/shard_map/psum | solution.py:12
  114.2 0.0 copy-done
  114.2 0.0 copy-start.7
  114.2 1.1 fusion.8
  115.3 0.0 copy-done.7
  115.3 0.0 copy-start.6
  115.3 0.2 convolution_add_fusion.6
  115.5 0.7 copy-done.6
  116.2 0.0 copy-start.5
  116.2 0.2 convolution_add_fusion.5
  116.4 0.7 copy-done.5
  117.1 0.0 copy-start.4
  117.1 0.2 convolution_add_fusion.4
  117.3 0.7 copy-done.4
  118.0 0.0 copy-start.3
  118.0 0.2 convolution_add_fusion.3
  118.2 0.7 copy-done.3
  118.9 0.0 copy-start.2
  118.9 0.2 convolution_add_fusion.2
  119.1 0.7 copy-done.2
  119.8 0.0 copy-start.1
  119.8 0.2 convolution_add_fusion.1
  120.0 0.7 copy-done.1
  120.7 0.9 fusion
  121.6 0.0 reduce-scatter.3.cloned.1.call-update
  121.6 0.0 reduce-scatter.5.cloned.1.call-start
  121.7 11.2 %reduce-scatter.3.cloned.1.call-done = f32[128,256]{0,1:T(8,128)} async-done(((f32[128,512]{0,1:T(8,128)}), f32[128,256]{0,1:T(8,128)}) %reduce-scatter.3.cloned.1.call-update) | async-done | bytes 131088 | tf_op jit(solution)/shard_map/reduce_scatter | solution.py:32
  132.9 1.6 select_convert_fusion
  134.4 1.0 fusion.11
  135.5 0.0 reduce-scatter.5.cloned.1.call-update
  135.5 0.0 copy-start.8
  135.5 0.7 copy.7
  136.2 56.4 %reduce-scatter.5.cloned.1.call-done = f32[32,256]{1,0:T(8,128)} async-done(((f32[512,256]{1,0:T(8,128)}), f32[32,256]{1,0:T(8,128)}) %reduce-scatter.5.cloned.1.call-update) | async-done | bytes 32784 | tf_op jit(solution)/shard_map/reduce_scatter | solution.py:40
  192.7 0.0 copy-done.8
  192.7 1.4 sub.5
Async XLA Ops:
  7.2 107.0 %all-reduce.3.cloned.1.call-start = ((), (), s32[]{:S(2)}) async-start(), calls=%async_computation.4 | async-start | bytes 2097152 | tf_op jit(solution)/shard_map/psum | solution.py:12
  8.2 0.7 copy-start.9
  17.0 97.2 %copy-start = (bf16[128,1024]{1,0:T(8,128)(2,1)S(1)}, bf16[128,1024]{1,0:T(8,128)(2,1)}, u32[]{:S(2)}) copy-start(bf16[128,1024]{1,0:T(8,128)(2,1)} %param.4) | copy-start | bytes 786436
  17.0 115.9 %reduce-scatter.3.cloned.1.call-start = ((), (), s32[]{:S(2)}) async-start(), calls=%async_computation.2 | async-start | bytes 393216 | tf_op jit(solution)/shard_map/reduce_scatter | solution.py:32
  114.2 1.1 copy-start.7
  115.3 0.9 copy-start.6
  116.2 0.9 copy-start.5
  117.1 0.9 copy-start.4
  118.0 0.9 copy-start.3
  118.9 0.9 copy-start.2
  119.8 0.9 copy-start.1
  121.6 71.0 %reduce-scatter.5.cloned.1.call-start = ((), (), s32[]{:S(2)}) async-start(), calls=%async_computation.3 | async-start | bytes 557056 | tf_op jit(solution)/shard_map/reduce_scatter | solution.py:40
  135.5 57.2 %copy-start.8 = (f32[32,256]{1,0:T(8,128)S(1)}, f32[32,256]{1,0:T(8,128)}, u32[]{:S(2)}) copy-start(f32[32,256]{1,0:T(8,128)} %param.6) | copy-start | bytes 98308
Sparse Core Ops, SparseCore 0:
  17.1 96.9 all-reduce.2
  121.8 11.0 reduce-scatter.2
  136.4 56.2 reduce-scatter.4
where the time goes:
time: 201 us
  waiting for transfers between devices  165 us (82%)
  between operations  13.9 us (7%)
  local copies, waits for them, and re-layouts  6.57 us (3%)
  blocking collectives  5.89 us (3%)
  other arithmetic  5.18 us (3%)
  matrix products  4.18 us (2%)
    psum x1, waiting for transfers between devices, broadcast(): return lax.psum(jnp.where(mine, array, jnp.zeros_like(array)), axis)  97.1 us
    reduce_scatter x1, waiting for transfers between devices, shards(): lax.psum_scatter(partial_term, 'row', scatter_dimension=0, tiled=True)  56.4 us
    reduce_scatter x1, waiting for transfers between devices, shards(): lax.psum_scatter(running, 'col', scatter_dimension=1, tiled=True)  11.2 us
    unnamed x22, local copies, waits for them, and re-layouts  6.57 us
    all_gather x1, blocking collectives, shards(): whole_rows = lax.all_gather(masked, 'col', axis=1, tiled=True)  5.89 us
  transfers between devices with their start and end apart: 3, of which 3 were waited for; matrix products, arithmetic and copies ran while one was open for 0% of the time, Pallas kernels for 0%

commit v1 on v0

v1 whole, which is shorter than its diff:
```python
import functools

import jax
import jax.numpy as jnp
from jax import lax
from jax.experimental import pallas as pl
from jax.experimental.pallas import tpu as pltpu
from jax.sharding import PartitionSpec as P

MESH = pl.DeviceIdType.MESH
UP, DOWN, ACROSS, PARTNER = range(4)


def kernel(
    rows, cols, group,
    pattern_ref, inv_ref, pan_ref, diag_ref,
    off_ref, out_ref,
    inv_buf, pan_buf, mate, terms, pair_buf, sums, red_buf,
    local_sem, pan_send, pan_recv, inv_send, inv_recv, mate_send, mate_recv,
    pair_send, pair_recv, red_send, red_recv,
):
    row = lax.axis_index("row")
    col = lax.axis_index("col")
    core = row % 2
    side = (row // 2) % 2
    layer = row // 4
    layers = rows // 4
    chips = rows // 2
    chip = row // 2
    partner = row + 1 - 2 * core
    across = row + 2 - 4 * side
    place = col % group
    supernode = col // group
    has_up = layer < layers - 1
    has_down = layer > 0
    height, half = pan_ref.shape

    own_inv = pltpu.make_async_copy(inv_ref, inv_buf.at[col], local_sem.at[0])
    own_pan = pltpu.make_async_copy(pan_ref, pan_buf.at[row], local_sem.at[1])
    own_mate = pltpu.make_async_copy(pan_ref, mate.at[place], local_sem.at[2])
    own_inv.start()
    own_pan.start()
    own_mate.start()

    barrier = pltpu.get_barrier_semaphore()

    def greet(**where):
        pl.semaphore_signal(barrier, inc=1, device_id=where, device_id_type=MESH)

    greet(row=across)
    greet(row=partner)
    for step in range(1, cols):
        greet(col=(col + step) % cols)

    @pl.when(has_up)
    def _():
        greet(row=row + 4)

    @pl.when(has_down)
    def _():
        greet(row=row - 4)

    ends = (layer + layers - 1) // layers + (2 * layers - 2 - layer) // layers
    pl.semaphore_wait(barrier, 2 + cols - 1 + ends)

    pending = []

    def launch(copy, cond=None):
        if cond is None:
            copy.start()
        else:
            pl.when(cond)(copy.start)
        pending.append((cond, copy))

    def panel_copy(source, direction, src=None):
        target = {UP: row + 4, DOWN: row - 4, ACROSS: across, PARTNER: partner}[direction]
        return pltpu.make_async_remote_copy(
            src_ref=pan_buf.at[source] if src is None else src,
            dst_ref=pan_buf.at[source],
            send_sem=pan_send.at[source, direction],
            recv_sem=pan_recv.at[source],
            device_id={"row": target},
            device_id_type=MESH,
        )

    launch(panel_copy(row, ACROSS, pan_ref))
    launch(panel_copy(row, UP, pan_ref), has_up)
    launch(panel_copy(row, DOWN, pan_ref), has_down)
    launch(panel_copy(row, PARTNER, pan_ref))

    inv_copies = []
    for step in range(1, cols):
        copy = pltpu.make_async_remote_copy(
            src_ref=inv_ref,
            dst_ref=inv_buf.at[col],
            send_sem=inv_send.at[step],
            recv_sem=inv_recv.at[step],
            device_id={"col": (col + step) % cols},
            device_id_type=MESH,
        )
        launch(copy)
        inv_copies.append(copy)
    mate_copies = []
    for step in range(1, group):
        copy = pltpu.make_async_remote_copy(
            src_ref=pan_ref,
            dst_ref=mate.at[place],
            send_sem=mate_send.at[step],
            recv_sem=mate_recv.at[step],
            device_id={"col": supernode * group + (place + step) % group},
            device_id_type=MESH,
        )
        launch(copy)
        mate_copies.append(copy)

    def arrive(source, onward, cond=None):
        def take():
            panel_copy(source, PARTNER).wait_recv()

        if cond is None:
            take()
        else:
            pl.when(cond)(take)
        for direction, also in onward:
            both = cond if also is None else (also if cond is None else cond & also)
            launch(panel_copy(source, direction), both)

    def arrive_across(distance):
        if distance == 0:
            arrive(across, [(PARTNER, None)])
        else:
            arrive(across - 4 * distance, [(PARTNER, None)], layer >= distance)
            arrive(across + 4 * distance, [(PARTNER, None)], layer < layers - distance)

    for distance in range(1, layers):
        arrive(
            row - 4 * distance,
            [(UP, has_up), (ACROSS, None), (PARTNER, None)],
            layer >= distance,
        )
        arrive(
            row + 4 * distance,
            [(DOWN, has_down), (ACROSS, None), (PARTNER, None)],
            layer < layers - distance,
        )
        arrive_across(distance - 1)
    arrive_across(layers - 1)

    for index in range(chips):
        panel_copy(2 * index + 1 - core, PARTNER).wait_recv()
    own_inv.wait()
    own_pan.wait()

    per_col = rows // cols
    total = jnp.zeros((height, half), jnp.float32)
    for step in range(cols):
        owner = (col + cols - step) % cols
        if step:
            inv_copies[step - 1].wait_recv()
        parts = []
        for index in range(per_col):
            block = inv_buf[owner, :, index * height : (index + 1) * height]
            live = pattern_ref[supernode, owner * per_col + index] > 0
            parts.append(jnp.where(live, block, jnp.zeros_like(block)))
        panel = pan_buf[pl.ds(owner * per_col, per_col)].reshape(per_col * height, half)
        total += jnp.dot(
            jnp.concatenate(parts, axis=1), panel, preferred_element_type=jnp.float32
        )
    own_live = pattern_ref[supernode, row] > 0
    offdiag = jnp.where(own_live, -total, jnp.zeros_like(total)).astype(jnp.bfloat16)
    off_ref[...] = offdiag

    own_mate.wait()
    for copy in mate_copies:
        copy.wait_recv()
    pairs = chips // group
    for index in range(group):
        term = lax.dot_general(
            mate[index], offdiag, (((0,), (0,)), ((), ())), preferred_element_type=jnp.float32
        )
        terms[index * pairs : (index + 1) * pairs] = term.reshape(pairs, *terms.shape[1:])

    pair_copy = pltpu.make_async_remote_copy(
        src_ref=terms.at[:, 1 - core],
        dst_ref=pair_buf,
        send_sem=pair_send,
        recv_sem=pair_recv,
        device_id={"row": partner},
        device_id_type=MESH,
    )
    launch(pair_copy)
    pair_copy.wait_recv()
    sums[...] = terms[:, core] + pair_buf[...]
    red_copies = []
    for step in range(1, chips):
        target = (chip + step) % chips
        copy = pltpu.make_async_remote_copy(
            src_ref=sums.at[target],
            dst_ref=red_buf.at[chip],
            send_sem=red_send.at[step],
            recv_sem=red_recv.at[step],
            device_id={"row": 2 * target + core},
            device_id_type=MESH,
        )
        launch(copy)
        red_copies.append(copy)
    result = sums[chip]
    for step in range(1, chips):
        red_copies[step - 1].wait_recv()
        result += red_buf[(chip + chips - step) % chips]
    out_ref[...] = diag_ref[...] - result

    for cond, copy in pending:
        if cond is None:
            copy.wait_send()
        else:
            pl.when(cond)(copy.wait_send)


def shards(rows, cols, inverse_rows, panel_rows, diag_inverse, pattern):
    height, half = panel_rows.shape
    chunk = diag_inverse.shape[0]
    group = rows * chunk // half
    chips = rows // 2
    dma = pltpu.SemaphoreType.DMA
    vmem = pl.BlockSpec(memory_space=pltpu.VMEM)
    anywhere = pl.BlockSpec(memory_space=pl.ANY)
    offdiag, diag_block = pl.pallas_call(
        functools.partial(kernel, rows, cols, group),
        out_shape=(
            jax.ShapeDtypeStruct((height, half), jnp.bfloat16),
            jax.ShapeDtypeStruct((chunk, half), jnp.float32),
        ),
        in_specs=[pl.BlockSpec(memory_space=pltpu.SMEM), anywhere, anywhere, vmem],
        out_specs=(vmem, vmem),
        scratch_shapes=[
            pltpu.VMEM((cols, *inverse_rows.shape), jnp.bfloat16),
            pltpu.VMEM((rows, height, half), jnp.bfloat16),
            pltpu.VMEM((group, height, half), jnp.bfloat16),
            pltpu.VMEM((chips, 2, chunk, half), jnp.float32),
            pltpu.VMEM((chips, chunk, half), jnp.float32),
            pltpu.VMEM((chips, chunk, half), jnp.float32),
            pltpu.VMEM((chips, chunk, half), jnp.float32),
            dma((3,)),
            dma((rows, 4)),
            dma((rows,)),
            dma((cols,)),
            dma((cols,)),
            dma((group,)),
            dma((group,)),
            dma,
            dma,
            dma((chips,)),
            dma((chips,)),
        ],
        compiler_params=pltpu.CompilerParams(
            collective_id=0, has_side_effects=True, vmem_limit_bytes=48 * 1024 * 1024
        ),
    )(pattern, inverse_rows, panel_rows, diag_inverse)
    return offdiag, diag_block


def solution(mesh):
    placed = (P("row", "col"), P("row", "col"), P("row", "col"), P())
    return jax.shard_map(
        functools.partial(shards, mesh.shape["row"], mesh.shape["col"]),
        mesh=mesh,
        in_specs=placed,
        out_specs=(P("row", "col"), P("row", "col")),
        check_vma=False,
    )
```

time: 201 us -> 32.2 us (0.16)
  waiting for transfers between devices: 165 us -> 0 us
  Pallas kernels: 0 us -> 26.9 us
  between operations: 13.9 us -> 0.65 us
  blocking collectives: 5.89 us -> 0 us
  other arithmetic: 5.18 us -> 0 us
  matrix products: 4.18 us -> 0 us
  local copies, waits for them, and re-layouts: 6.57 us -> 4.44 us
    psum x1 -> x0, waiting for transfers between devices: 97.1 us -> none  [broadcast(): return lax.psum(jnp.where(mine, array, jnp.zeros_like(array)), axis)]
    reduce_scatter x2 -> x0, waiting for transfers between devices: 67.6 us -> none  [the longest x1 56.4 us: shards(): lax.psum_scatter(partial_term, 'row', scatter_dimension=0, tiled=True)]
    pallas_call x0 -> x1, Pallas kernels: none -> 26.9 us  [shards(): pl.pallas_call(functools.partial(kernel, rows, cols, group), out_shape=(j...]
    all_gather x1 -> x0, blocking collectives: 5.89 us -> none  [shards(): whole_rows = lax.all_gather(masked, 'col', axis=1, tiled=True)]
    dot_general x9 -> x0, matrix products: 4.18 us -> none  [the longest x8 3.16 us: shards(): jnp.dot(columns, received, preferred_element_type=jnp.float32)]
    unnamed x22 -> x10, local copies, waits for them, and re-layouts: 6.57 us -> 4.44 us
  transfers between devices with their start and end apart: 3 -> 0, of which waited for: 3 -> 0; matrix products, arithmetic and copies ran while one was open for 0% -> 0% of each run, Pallas kernels for 0% -> 0%
where the time goes in v1:
time: 32.2 us; the launch traced here: 32 us
  Pallas kernels  26.9 us (84%)
  local copies, waits for them, and re-layouts  4.44 us (14%)
  between operations  0.65 us (2%)
    pallas_call x1, Pallas kernels, shards(): pl.pallas_call(functools.partial(kernel, rows, cols, group), out_shape=(j...  26.9 us
    unnamed x10, local copies, waits for them, and re-layouts  4.44 us

profile of v1, /device:TPU:0, one launch (start us, length us, event | category | flops | bytes accessed | tf_op | source)
XLA Modules:
  0.0 32.0 jit_solution(7186285669552178158)
XLA Ops:
  0.6 0.0 copy-start
  0.6 0.9 %copy-done = bf16[128,1024]{1,0:T(8,128)(2,1)S(1)} copy-done((bf16[128,1024]{1,0:T(8,128)(2,1)S(1)}, bf16[128,1024]{1,0:T(8,128)(2,1)}, u32[]{:S(2)}) %copy-start) | copy-done | bytes 262168
  1.6 0.0 copy-start.1
  1.6 0.8 %copy-done.1 = bf16[128,256]{1,0:T(8,128)(2,1)S(1)} copy-done((bf16[128,256]{1,0:T(8,128)(2,1)S(1)}, bf16[128,256]{1,0:T(8,128)(2,1)}, u32[]{:S(2)}) %copy-start.1) | copy-done | bytes 65560
  2.4 0.0 copy-start.2
  2.4 0.8 %copy-done.2 = f32[32,256]{1,0:T(8,128)S(1)} copy-done((f32[32,256]{1,0:T(8,128)S(1)}, f32[32,256]{1,0:T(8,128)}, u32[]{:S(2)}) %copy-start.2) | copy-done | bytes 32792
  3.2 0.0 copy-start.3
  3.2 0.7 %copy-done.3 = s32[1,16]{1,0:T(1,128)S(1)} copy-done((s32[1,16]{1,0:T(1,128)S(1)}, s32[1,16]{1,0:T(1,128)}, u32[]{:S(2)}) %copy-start.3) | copy-done | bytes 88
  3.8 26.9 %shard_map.59 = (bf16[128,256]{1,0:T(8,128)(2,1)S(1)}, f32[32,256]{1,0:T(8,128)S(1)}) custom-call(s32[1,16]{1,0:T(1,128)S(1)} %copy-done.3, bf16[128,1024]{1,0:T(8,128)(2,1)S(1)} %copy-done, bf16[128,256]{1,0:T(8,128)(2,1)S(1)} %copy-done.1, f32[32,256]{1,0:T(8,128)S(1)} %copy-done.2), custom_call_target="tpu_custom_call" | custom-call | tf_op jit(solution)/shard_map/pallas_call | solution.py:228
  30.7 0.6 %copy.8 = bf16[128,256]{1,0:T(8,128)(2,1)} copy(bf16[128,256]{1,0:T(8,128)(2,1)S(1)} %get-tuple-element.4) | data formatting | bytes 131072
  31.3 0.6 %copy.9 = f32[32,256]{1,0:T(8,128)} copy(f32[32,256]{1,0:T(8,128)S(1)} %get-tuple-element.5) | data formatting | bytes 65536
Async XLA Ops:
  0.6 1.0 %copy-start = (bf16[128,1024]{1,0:T(8,128)(2,1)S(1)}, bf16[128,1024]{1,0:T(8,128)(2,1)}, u32[]{:S(2)}) copy-start(bf16[128,1024]{1,0:T(8,128)(2,1)} %inv_ref.1) | copy-start | bytes 786436
  1.6 0.8 %copy-start.1 = (bf16[128,256]{1,0:T(8,128)(2,1)S(1)}, bf16[128,256]{1,0:T(8,128)(2,1)}, u32[]{:S(2)}) copy-start(bf16[128,256]{1,0:T(8,128)(2,1)} %pan_ref.1) | copy-start | bytes 196612
  2.4 0.8 %copy-start.2 = (f32[32,256]{1,0:T(8,128)S(1)}, f32[32,256]{1,0:T(8,128)}, u32[]{:S(2)}) copy-start(f32[32,256]{1,0:T(8,128)} %diag_ref.1) | copy-start | bytes 98308
  3.2 0.7 %copy-start.3 = (s32[1,16]{1,0:T(1,128)S(1)}, s32[1,16]{1,0:T(1,128)}, u32[]{:S(2)}) copy-start(s32[1,16]{1,0:T(1,128)} %pattern_ref.1) | copy-start | bytes 196

commit v2 on v1

--- a/solution.py
+++ b/solution.py
@@ -8,14 +8,15 @@
 from jax.sharding import PartitionSpec as P
 
 MESH = pl.DeviceIdType.MESH
+SPLIT = 1
 UP, DOWN, ACROSS, PARTNER = range(4)
 
 
 def kernel(
     rows, cols, group,
-    pattern_ref, inv_ref, pan_ref, diag_ref,
+    pattern_hbm, inv_ref, pan_ref, diag_hbm,
     off_ref, out_ref,
-    inv_buf, pan_buf, mate, terms, pair_buf, sums, red_buf,
+    pattern_ref, diag_ref, inv_buf, pan_buf, mate, terms, pair_buf, sums, red_buf,
     local_sem, pan_send, pan_recv, inv_send, inv_recv, mate_send, mate_recv,
     pair_send, pair_recv, red_send, red_recv,
 ):
@@ -38,6 +39,10 @@
     own_inv = pltpu.make_async_copy(inv_ref, inv_buf.at[col], local_sem.at[0])
     own_pan = pltpu.make_async_copy(pan_ref, pan_buf.at[row], local_sem.at[1])
     own_mate = pltpu.make_async_copy(pan_ref, mate.at[place], local_sem.at[2])
+    own_pattern = pltpu.make_async_copy(pattern_hbm, pattern_ref, local_sem.at[3])
+    own_diag = pltpu.make_async_copy(diag_hbm, diag_ref, local_sem.at[4])
+    own_pattern.start()
+    own_diag.start()
     own_inv.start()
     own_pan.start()
     own_mate.start()
@@ -72,21 +77,25 @@
             pl.when(cond)(copy.start)
         pending.append((cond, copy))
 
-    def panel_copy(source, direction, src=None):
+    piece = height // SPLIT
+
+    def panel_copy(source, part, direction, own=False):
         target = {UP: row + 4, DOWN: row - 4, ACROSS: across, PARTNER: partner}[direction]
+        lines = pl.ds(part * piece, piece)
         return pltpu.make_async_remote_copy(
-            src_ref=pan_buf.at[source] if src is None else src,
-            dst_ref=pan_buf.at[source],
-            send_sem=pan_send.at[source, direction],
-            recv_sem=pan_recv.at[source],
+            src_ref=pan_ref.at[lines] if own else pan_buf.at[source, lines],
+            dst_ref=pan_buf.at[source, lines],
+            send_sem=pan_send.at[source, part, direction],
+            recv_sem=pan_recv.at[source, part],
             device_id={"row": target},
             device_id_type=MESH,
         )
 
-    launch(panel_copy(row, ACROSS, pan_ref))
-    launch(panel_copy(row, UP, pan_ref), has_up)
-    launch(panel_copy(row, DOWN, pan_ref), has_down)
-    launch(panel_copy(row, PARTNER, pan_ref))
+    for part in range(SPLIT):
+        launch(panel_copy(row, part, UP, True), has_up)
+        launch(panel_copy(row, part, DOWN, True), has_down)
+        launch(panel_copy(row, part, ACROSS, True))
+        launch(panel_copy(row, part, PARTNER, True))
 
     inv_copies = []
     for step in range(1, cols):
@@ -113,41 +122,43 @@
         launch(copy)
         mate_copies.append(copy)
 
-    def arrive(source, onward, cond=None):
-        def take():
-            panel_copy(source, PARTNER).wait_recv()
-
+    def arrive(source, part, onward, cond=None):
+        take = panel_copy(source, part, PARTNER).wait_recv
         if cond is None:
             take()
         else:
             pl.when(cond)(take)
         for direction, also in onward:
-            both = cond if also is None else (also if cond is None else cond & also)
-            launch(panel_copy(source, direction), both)
-
-    def arrive_across(distance):
-        if distance == 0:
-            arrive(across, [(PARTNER, None)])
-        else:
-            arrive(across - 4 * distance, [(PARTNER, None)], layer >= distance)
-            arrive(across + 4 * distance, [(PARTNER, None)], layer < layers - distance)
-
-    for distance in range(1, layers):
-        arrive(
-            row - 4 * distance,
-            [(UP, has_up), (ACROSS, None), (PARTNER, None)],
-            layer >= distance,
-        )
-        arrive(
-            row + 4 * distance,
-            [(DOWN, has_down), (ACROSS, None), (PARTNER, None)],
-            layer < layers - distance,
-        )
-        arrive_across(distance - 1)
-    arrive_across(layers - 1)
+            both = cond if also is None else cond & also
+            launch(panel_copy(source, part, direction), both)
+
+    for distance in range(1, layers + 1):
+        for part in range(SPLIT):
+            if distance < layers:
+                arrive(
+                    row - 4 * distance,
+                    part,
+                    [(UP, has_up), (ACROSS, None), (PARTNER, None)],
+                    layer >= distance,
+                )
+                arrive(
+                    row + 4 * distance,
+                    part,
+                    [(DOWN, has_down), (ACROSS, None), (PARTNER, None)],
+                    layer < layers - distance,
+                )
+            far = distance - 1
+            onward = [(PARTNER, None)]
+            if far == 0:
+                arrive(across, part, onward)
+            else:
+                arrive(across - 4 * far, part, onward, layer >= far)
+                arrive(across + 4 * far, part, onward, layer < layers - far)
 
     for index in range(chips):
-        panel_copy(2 * index + 1 - core, PARTNER).wait_recv()
+        for part in range(SPLIT):
+            panel_copy(2 * index + 1 - core, part, PARTNER).wait_recv()
+    own_pattern.wait()
     own_inv.wait()
     own_pan.wait()
 
@@ -204,6 +215,7 @@
         )
         launch(copy)
         red_copies.append(copy)
+    own_diag.wait()
     result = sums[chip]
     for step in range(1, chips):
         red_copies[step - 1].wait_recv()
@@ -215,6 +227,15 @@
             copy.wait_send()
         else:
             pl.when(cond)(copy.wait_send)
+
+
+def write_out(off_ref, diag_ref, off_out, diag_out, sem):
+    first = pltpu.make_async_copy(off_ref, off_out, sem.at[0])
+    second = pltpu.make_async_copy(diag_ref, diag_out, sem.at[1])
+    first.start()
+    second.start()
+    first.wait()
+    second.wait()
 
 
 def shards(rows, cols, inverse_rows, panel_rows, diag_inverse, pattern):
@@ -224,16 +245,19 @@
     chips = rows // 2
     dma = pltpu.SemaphoreType.DMA
     vmem = pl.BlockSpec(memory_space=pltpu.VMEM)
-    anywhere = pl.BlockSpec(memory_space=pl.ANY)
+    hbm = pl.BlockSpec(memory_space=pltpu.HBM)
+    operands = (pattern, inverse_rows, panel_rows, diag_inverse)
     offdiag, diag_block = pl.pallas_call(
         functools.partial(kernel, rows, cols, group),
         out_shape=(
             jax.ShapeDtypeStruct((height, half), jnp.bfloat16),
             jax.ShapeDtypeStruct((chunk, half), jnp.float32),
         ),
-        in_specs=[pl.BlockSpec(memory_space=pltpu.SMEM), anywhere, anywhere, vmem],
+        in_specs=[hbm, hbm, hbm, hbm],
         out_specs=(vmem, vmem),
         scratch_shapes=[
+            pltpu.SMEM(pattern.shape, jnp.int32),
+            pltpu.VMEM(diag_inverse.shape, jnp.float32),
             pltpu.VMEM((cols, *inverse_rows.shape), jnp.bfloat16),
             pltpu.VMEM((rows, height, half), jnp.bfloat16),
             pltpu.VMEM((group, height, half), jnp.bfloat16),
@@ -241,9 +265,9 @@
             pltpu.VMEM((chips, chunk, half), jnp.float32),
             pltpu.VMEM((chips, chunk, half), jnp.float32),
             pltpu.VMEM((chips, chunk, half), jnp.float32),
-            dma((3,)),
-            dma((rows, 4)),
-            dma((rows,)),
+            dma((5,)),
+            dma((rows, SPLIT, 4)),
+            dma((rows, SPLIT)),
             dma((cols,)),
             dma((cols,)),
             dma((group,)),
@@ -256,8 +280,18 @@
         compiler_params=pltpu.CompilerParams(
             collective_id=0, has_side_effects=True, vmem_limit_bytes=48 * 1024 * 1024
         ),
-    )(pattern, inverse_rows, panel_rows, diag_inverse)
-    return offdiag, diag_block
+    )(*(pltpu.with_memory_space_constraint(given, pltpu.HBM) for given in operands))
+    return pl.pallas_call(
+        write_out,
+        out_shape=(
+            jax.ShapeDtypeStruct((height, half), jnp.bfloat16),
+            jax.ShapeDtypeStruct((chunk, half), jnp.float32),
+        ),
+        in_specs=[vmem, vmem],
+        out_specs=(hbm, hbm),
+        scratch_shapes=[dma((2,))],
+        compiler_params=pltpu.CompilerParams(vmem_limit_bytes=1024 * 1024),
+    )(offdiag, diag_block)
 
 
 def solution(mesh):

time: 32.2 us -> 27.9 us (0.87)
  local copies, waits for them, and re-layouts: 4.44 us -> 0 us
    unnamed x10 -> x0, local copies, waits for them, and re-layouts: 4.44 us -> none
    pallas_call x0 -> x1, Pallas kernels: none -> 0.66 us  [shards(): pl.pallas_call(write_out, out_shape=(jax.ShapeDtypeStruct((height, half),...]
    pallas_call x1, Pallas kernels: 26.9 us -> 26.4 us  [shards(): pl.pallas_call(functools.partial(kernel, rows, cols, group), out_shape=(j...]
where the time goes in v2:
time: 27.9 us; the launch traced here: 27.7 us
  Pallas kernels  27.1 us (97%)
  between operations  0.64 us (2%)
    pallas_call x1, Pallas kernels, shards(): pl.pallas_call(functools.partial(kernel, rows, cols, group), out_shape=(j...  26.4 us
    pallas_call x1, Pallas kernels, shards(): pl.pallas_call(write_out, out_shape=(jax.ShapeDtypeStruct((height, half),...  0.66 us

profile of v2, /device:TPU:0, one launch (start us, length us, event | category | flops | bytes accessed | tf_op | source)
XLA Modules:
  0.0 27.7 jit_solution(15856616516944226311)
XLA Ops:
  0.6 26.4 %shard_map.59 = (bf16[128,256]{1,0:T(8,128)(2,1)S(1)}, f32[32,256]{1,0:T(8,128)S(1)}) custom-call(s32[1,16]{1,0:T(1,128)} %pattern_hbm.1, bf16[128,1024]{1,0:T(8,128)(2,1)} %inv_ref.1, bf16[128,256]{1,0:T(8,128)(2,1)} %pan_ref.1, f32[32,256]{1,0:T(8,128)} %diag_hbm.1), custom_call_target="tpu_custom_call" | custom-call | tf_op jit(solution)/shard_map/pallas_call | solution.py:250
  27.1 0.7 %shard_map.60 = (bf16[128,256]{1,0:T(8,128)(2,1)}, f32[32,256]{1,0:T(8,128)}) custom-call(bf16[128,256]{1,0:T(8,128)(2,1)S(1)} %get-tuple-element.4.off_ref, f32[32,256]{1,0:T(8,128)S(1)} %get-tuple-element.5.diag_ref), custom_call_target="tpu_custom_call" | custom-call | tf_op jit(solution)/shard_map/pallas_call | solution.py:284

commit v3 on v0

v3 whole, which is shorter than its diff:
```python
import functools

import jax
import jax.numpy as jnp
from jax import lax
from jax.experimental import pallas as pl
from jax.experimental.pallas import tpu as pltpu
from jax.sharding import PartitionSpec as P

MESH = pl.DeviceIdType.MESH


def kernel(
    rows, cols, group,
    pattern_hbm, inv_ref, pan_ref, diag_hbm,
    off_ref, out_ref,
    pattern_ref, diag_ref, inv_buf, pan_buf, mate, off_far, off_in, terms, red_buf,
    local_sem, own_send, fwd_send, pan_recv, inv_send, inv_recv, mate_send, mate_recv,
    off_send, off_recv, red_send, red_recv,
):
    row = lax.axis_index("row")
    col = lax.axis_index("col")
    core = row % 2
    side = (row // 2) % 2
    layer = row // 4
    layers = rows // 4
    partner = row + 1 - 2 * core
    across = row + 2 - 4 * side
    place = col % group
    supernode = col // group
    height, half = pan_ref.shape
    quarter = half // 2

    def lanes(which):
        return pl.ds(pl.multiple_of(which * quarter, quarter), quarter)

    near, other = lanes(core), lanes(1 - core)

    local = [
        pltpu.make_async_copy(src, dst, local_sem.at[index])
        for index, (src, dst) in enumerate(
            [
                (pattern_hbm, pattern_ref),
                (diag_hbm, diag_ref),
                (pan_ref, mate.at[place, 0]),
                (pan_ref.at[:, near], pan_buf.at[row]),
                (inv_ref, inv_buf.at[col, 0]),
            ]
        )
    ]
    for copy in local:
        copy.start()

    barrier = pltpu.get_barrier_semaphore()

    def greet(**where):
        pl.semaphore_signal(barrier, inc=1, device_id=where, device_id_type=MESH)

    greet(row=partner)
    for base in (row, partner):
        greet(row=base + 2 - 4 * side)
        for step in range(1, layers):
            greet(row=(base + 4 * step) % rows)
    for step in range(1, cols):
        greet(col=(col + step) % cols)
    pl.semaphore_wait(barrier, 2 * layers + cols)

    pending = []

    def launch(copy, cond=None):
        if cond is None:
            copy.start()
        else:
            pl.when(cond)(copy.start)
        pending.append((cond, copy))
        return copy

    def remote(src, dst, send, recv, **where):
        return pltpu.make_async_remote_copy(
            src_ref=src,
            dst_ref=dst,
            send_sem=send,
            recv_sem=recv,
            device_id=where,
            device_id_type=MESH,
        )

    def own_panel(slot, part, target):
        return remote(
            pan_ref.at[:, part], pan_buf.at[row], own_send.at[slot], pan_recv.at[row], row=target
        )

    def passed_on(source):
        return remote(
            pan_buf.at[source], pan_buf.at[source], fwd_send.at[source], pan_recv.at[source],
            row=across,
        )

    sides = ((0, near, row), (1, other, partner))
    for slot, part, base in sides:
        launch(own_panel(slot, part, base + 2 - 4 * side))
    for far in range(1, layers):
        for slot, part, base in sides:
            slot = 4 * far + 2 * slot
            launch(own_panel(slot, part, base + 4 * far), layer < layers - far)
            launch(own_panel(slot + 1, part, base - 4 * far), layer >= far)
    launch(own_panel(2, other, partner))

    inv_copies, mate_copies = [], []
    for step in range(1, cols):
        inv_copies.append(
            launch(
                remote(
                    inv_ref, inv_buf.at[col, 0], inv_send.at[step, 0], inv_recv.at[step, 0],
                    col=(col + step) % cols,
                )
            )
        )
    for step in range(1, group):
        mate_copies.append(
            launch(
                remote(
                    pan_ref, mate.at[place, 0], mate_send.at[step, 0], mate_recv.at[step, 0],
                    col=supernode * group + (place + step) % group,
                )
            )
        )

    def share_inv(step):
        owner = (col + cols - step) % cols
        return remote(
            inv_buf.at[owner, 0] if step else inv_ref, inv_buf.at[owner, 1],
            inv_send.at[step, 1], inv_recv.at[step, 1], row=partner,
        )

    def share_mate(step):
        owner = (place + group - step) % group
        return remote(
            mate.at[owner, 0] if step else pan_ref, mate.at[owner, 1],
            mate_send.at[step, 1], mate_recv.at[step, 1], row=partner,
        )

    launch(share_inv(0))
    launch(share_mate(0))

    def arrive(source, cond, onward):
        if cond is None:
            passed_on(source).wait_recv()
        else:
            pl.when(cond)(passed_on(source).wait_recv)
        if onward:
            launch(passed_on(source), cond)

    for far in range(1, layers):
        for base in (row, partner):
            arrive(base - 4 * far, layer >= far, True)
            arrive(base + 4 * far, layer < layers - far, True)
    for step in range(1, cols):
        inv_copies[step - 1].wait_recv()
        launch(share_inv(step))
    for step in range(1, group):
        mate_copies[step - 1].wait_recv()
        launch(share_mate(step))
    arrive(partner, None, False)
    for base in (across, partner + 2 - 4 * side):
        arrive(base, None, False)
        for far in range(1, layers):
            arrive(base - 4 * far, layer >= far, False)
            arrive(base + 4 * far, layer < layers - far, False)
    for copy in local:
        copy.wait()
    for step in range(cols):
        share_inv(step).wait_recv()
    for step in range(group):
        share_mate(step).wait_recv()

    per_col = rows // cols
    total = jnp.zeros((2 * height, quarter), jnp.float32)
    for owner in range(cols):
        parts = []
        for index in range(per_col):
            block = inv_buf[owner, :, :, index * height : (index + 1) * height]
            block = block.reshape(2 * height, height)
            live = pattern_ref[supernode, owner * per_col + index] > 0
            parts.append(jnp.where(live, block, jnp.zeros_like(block)))
        panel = pan_buf[owner * per_col : (owner + 1) * per_col].reshape(-1, quarter)
        total += jnp.dot(
            jnp.concatenate(parts, axis=1), panel, preferred_element_type=jnp.float32
        )

    def kept(sums, which):
        live = pattern_ref[supernode, which] > 0
        return jnp.where(live, -sums, jnp.zeros_like(sums)).astype(jnp.bfloat16)

    off_own = kept(total[:height], row)
    off_other = kept(total[height:], partner)
    off_far[...] = off_other
    offdiag = jnp.concatenate([off_own, off_other], axis=0)
    span = rows // group
    for index in range(group):
        left = mate[index].reshape(2 * height, half)
        term = lax.dot_general(
            left, offdiag, (((0,), (0,)), ((), ())), preferred_element_type=jnp.float32
        )
        terms[index * span : (index + 1) * span] = term.reshape(span, *terms.shape[1:])

    red_copies = {}
    order = sorted(range(1, rows), key=lambda step: -min(step, rows - step))
    for step in order:
        target = (row + step) % rows
        red_copies[step] = launch(
            remote(
                terms.at[target], red_buf.at[row], red_send.at[step], red_recv.at[step],
                row=target,
            )
        )
    off_copy = launch(remote(off_far, off_in, off_send, off_recv, row=partner))
    off_ref[:, near] = off_own
    off_copy.wait_recv()
    off_ref[:, other] = off_in[...]
    results = [terms[row], None]
    for step in reversed(order):
        red_copies[step].wait_recv()
        piece = red_buf[(row + rows - step) % rows]
        which = step % 2
        results[which] = piece if results[which] is None else results[which] + piece
    out_ref[:, near] = diag_ref[:, near] - results[0]
    out_ref[:, other] = diag_ref[:, other] - results[1]

    for cond, copy in pending:
        if cond is None:
            copy.wait_send()
        else:
            pl.when(cond)(copy.wait_send)


def write_out(off_ref, diag_ref, off_out, diag_out, sem):
    first = pltpu.make_async_copy(off_ref, off_out, sem.at[0])
    second = pltpu.make_async_copy(diag_ref, diag_out, sem.at[1])
    first.start()
    second.start()
    first.wait()
    second.wait()


def shards(rows, cols, inverse_rows, panel_rows, diag_inverse, pattern):
    height, half = panel_rows.shape
    chunk = diag_inverse.shape[0]
    group = rows * chunk // half
    dma = pltpu.SemaphoreType.DMA
    vmem = pl.BlockSpec(memory_space=pltpu.VMEM)
    hbm = pl.BlockSpec(memory_space=pltpu.HBM)
    operands = (pattern, inverse_rows, panel_rows, diag_inverse)
    offdiag, diag_block = pl.pallas_call(
        functools.partial(kernel, rows, cols, group),
        out_shape=(
            jax.ShapeDtypeStruct((height, half), jnp.bfloat16),
            jax.ShapeDtypeStruct((chunk, half), jnp.float32),
        ),
        in_specs=[hbm, hbm, hbm, hbm],
        out_specs=(vmem, vmem),
        scratch_shapes=[
            pltpu.SMEM(pattern.shape, jnp.int32),
            pltpu.VMEM(diag_inverse.shape, jnp.float32),
            pltpu.VMEM((cols, 2, *inverse_rows.shape), jnp.bfloat16),
            pltpu.VMEM((rows, height, half // 2), jnp.bfloat16),
            pltpu.VMEM((group, 2, height, half), jnp.bfloat16),
            pltpu.VMEM((height, half // 2), jnp.bfloat16),
            pltpu.VMEM((height, half // 2), jnp.bfloat16),
            pltpu.VMEM((rows, chunk, half // 2), jnp.float32),
            pltpu.VMEM((rows, chunk, half // 2), jnp.float32),
            dma((5,)),
            dma((rows,)),
            dma((rows,)),
            dma((rows,)),
            dma((cols, 2)),
            dma((cols, 2)),
            dma((group, 2)),
            dma((group, 2)),
            dma,
            dma,
            dma((rows,)),
            dma((rows,)),
        ],
        compiler_params=pltpu.CompilerParams(
            collective_id=0, has_side_effects=True, vmem_limit_bytes=48 * 1024 * 1024
        ),
    )(*(pltpu.with_memory_space_constraint(given, pltpu.HBM) for given in operands))
    return pl.pallas_call(
        write_out,
        out_shape=(
            jax.ShapeDtypeStruct((height, half), jnp.bfloat16),
            jax.ShapeDtypeStruct((chunk, half), jnp.float32),
        ),
        in_specs=[vmem, vmem],
        out_specs=(hbm, hbm),
        scratch_shapes=[dma((2,))],
        compiler_params=pltpu.CompilerParams(vmem_limit_bytes=1024 * 1024),
    )(offdiag, diag_block)


def solution(mesh):
    placed = (P("row", "col"), P("row", "col"), P("row", "col"), P())
    return jax.shard_map(
        functools.partial(shards, mesh.shape["row"], mesh.shape["col"]),
        mesh=mesh,
        in_specs=placed,
        out_specs=(P("row", "col"), P("row", "col")),
        check_vma=False,
    )
```

time: 201 us -> 27 us (0.13)
  waiting for transfers between devices: 165 us -> 0 us
  Pallas kernels: 0 us -> 26.2 us
  between operations: 13.9 us -> 0.64 us
  local copies, waits for them, and re-layouts: 6.57 us -> 0 us
  blocking collectives: 5.89 us -> 0 us
  other arithmetic: 5.18 us -> 0 us
  matrix products: 4.18 us -> 0 us
    psum x1 -> x0, waiting for transfers between devices: 97.1 us -> none  [broadcast(): return lax.psum(jnp.where(mine, array, jnp.zeros_like(array)), axis)]
    reduce_scatter x2 -> x0, waiting for transfers between devices: 67.6 us -> none  [the longest x1 56.4 us: shards(): lax.psum_scatter(partial_term, 'row', scatter_dimension=0, tiled=True)]
    pallas_call x0 -> x2, Pallas kernels: none -> 26.2 us  [the longest x1 25.6 us: shards(): pl.pallas_call(functools.partial(kernel, rows, cols, group), out_shape=(j...]
    unnamed x22 -> x0, local copies, waits for them, and re-layouts: 6.57 us -> none
    all_gather x1 -> x0, blocking collectives: 5.89 us -> none  [shards(): whole_rows = lax.all_gather(masked, 'col', axis=1, tiled=True)]
    dot_general x9 -> x0, matrix products: 4.18 us -> none  [the longest x8 3.16 us: shards(): jnp.dot(columns, received, preferred_element_type=jnp.float32)]
  transfers between devices with their start and end apart: 3 -> 0, of which waited for: 3 -> 0; matrix products, arithmetic and copies ran while one was open for 0% -> 0% of each run, Pallas kernels for 0% -> 0%
where the time goes in v3:
time: 27 us; the launch traced here: 26.9 us
  Pallas kernels  26.2 us (97%)
  between operations  0.64 us (2%)
    pallas_call x1, Pallas kernels, shards(): pl.pallas_call(functools.partial(kernel, rows, cols, group), out_shape=(j...  25.6 us
    pallas_call x1, Pallas kernels, shards(): pl.pallas_call(write_out, out_shape=(jax.ShapeDtypeStruct((height, half),...  0.66 us

profile of v3, /device:TPU:0, one launch (start us, length us, event | category | flops | bytes accessed | tf_op | source)
XLA Modules:
  0.0 26.9 jit_solution(5243935730923211329)
XLA Ops:
  0.6 25.6 %shard_map.59 = (bf16[128,256]{1,0:T(8,128)(2,1)S(1)}, f32[32,256]{1,0:T(8,128)S(1)}) custom-call(s32[1,16]{1,0:T(1,128)} %pattern_hbm.1, bf16[128,1024]{1,0:T(8,128)(2,1)} %inv_ref.1, bf16[128,256]{1,0:T(8,128)(2,1)} %pan_ref.1, f32[32,256]{1,0:T(8,128)} %diag_hbm.1), custom_call_target="tpu_custom_call" | custom-call | tf_op jit(solution)/shard_map/pallas_call | solution.py:254
  26.2 0.7 %shard_map.60 = (bf16[128,256]{1,0:T(8,128)(2,1)}, f32[32,256]{1,0:T(8,128)}) custom-call(bf16[128,256]{1,0:T(8,128)(2,1)S(1)} %get-tuple-element.4.off_ref, f32[32,256]{1,0:T(8,128)S(1)} %get-tuple-element.5.diag_ref), custom_call_target="tpu_custom_call" | custom-call | tf_op jit(solution)/shard_map/pallas_call | solution.py:289

commit v4 on v3

--- a/solution.py
+++ b/solution.py
@@ -205,7 +205,7 @@
         terms[index * span : (index + 1) * span] = term.reshape(span, *terms.shape[1:])
 
     red_copies = {}
-    order = sorted(range(1, rows), key=lambda step: -min(step, rows - step))
+    order = sorted(range(1, rows), key=lambda step: min(step, rows - step))
     for step in order:
         target = (row + step) % rows
         red_copies[step] = launch(

time: 27 us -> 25.6 us (0.948)
  Pallas kernels: 26.2 us -> 24.8 us
    pallas_call x1, Pallas kernels: 25.6 us -> 24.2 us  [shards(): pl.pallas_call(functools.partial(kernel, rows, cols, group), out_shape=(j...]
where the time goes in v4:
time: 25.6 us; the launch traced here: 25.4 us
  Pallas kernels  24.8 us (97%)
  between operations  0.64 us (2%)
    pallas_call x1, Pallas kernels, shards(): pl.pallas_call(functools.partial(kernel, rows, cols, group), out_shape=(j...  24.2 us
    pallas_call x1, Pallas kernels, shards(): pl.pallas_call(write_out, out_shape=(jax.ShapeDtypeStruct((height, half),...  0.66 us

profile of v4, /device:TPU:0, one launch (start us, length us, event | category | flops | bytes accessed | tf_op | source)
XLA Modules:
  0.0 25.4 jit_solution(14504230279013505268)
XLA Ops:
  0.6 24.2 %shard_map.59 = (bf16[128,256]{1,0:T(8,128)(2,1)S(1)}, f32[32,256]{1,0:T(8,128)S(1)}) custom-call(s32[1,16]{1,0:T(1,128)} %pattern_hbm.1, bf16[128,1024]{1,0:T(8,128)(2,1)} %inv_ref.1, bf16[128,256]{1,0:T(8,128)(2,1)} %pan_ref.1, f32[32,256]{1,0:T(8,128)} %diag_hbm.1), custom_call_target="tpu_custom_call" | custom-call | tf_op jit(solution)/shard_map/pallas_call | solution.py:254
  24.8 0.7 %shard_map.60 = (bf16[128,256]{1,0:T(8,128)(2,1)}, f32[32,256]{1,0:T(8,128)}) custom-call(bf16[128,256]{1,0:T(8,128)(2,1)S(1)} %get-tuple-element.4.off_ref, f32[32,256]{1,0:T(8,128)S(1)} %get-tuple-element.5.diag_ref), custom_call_target="tpu_custom_call" | custom-call | tf_op jit(solution)/shard_map/pallas_call | solution.py:289
